TPU v7x, 512 devices: a whole 4x4x16 slice. The times are simulated.
512 devices in a mesh: seq: 128 (over y, z, core), ch: 4 (over x).
Axes of the slice: x: 4, y: 4, z: 16, core: 2. Of those that a mesh axis runs over, the one named last changes fastest.
Arguments:
- qkv: bfloat16 [3, 16384, 2048], P(None, 'seq', 'ch'), may hold values from -6 to 6
- filt: float32 [16384, 2048], P('seq', 'ch'), may hold values from -0.1875 to 0.1875
- skip_gain: float32 [2048], P('ch'), may hold values from -4 to 4
- short_weight: float32 [3, 3, 2048], P(None, None, 'ch'), may hold values from -3.5 to 3.5
- w_out: bfloat16 [2048, 2048], P(None, 'ch'), may hold values from -0.125 to 0.125
- g_out: bfloat16 [16384, 2048], P('seq', 'ch'), may hold values from -6 to 6
Outputs:
- output: bfloat16 [16384, 2048], P('seq', 'ch')
- grad_qkv: bfloat16 [3, 16384, 2048], P(None, 'seq', 'ch')
- grad_filter: float32 [16384, 2048], P('seq', 'ch')
All inputs are finite; a program needn't handle non-finite values.
Results may differ from a plain program's by a relative error of at most 0.0049.
Values may be sent and summed in bfloat16 or wider, within the bound.
A program may use at most 64 MiB of HBM per device.

v0:
```python
import math
import jax
import jax.numpy as jnp
from jax import lax
from jax.sharding import PartitionSpec as P

HIGHEST = lax.Precision.HIGHEST
TWO_PI = 2.0 * math.pi


def passed_along(block, axis, distance):
    devices = range(lax.axis_size(axis))
    route = [(i - distance, i) for i in devices if i - distance in devices]
    return lax.ppermute(block, axis, route)


def phase_pair(left_count, right_count, period, left_start, right_start):
    left_idx = lax.broadcasted_iota(jnp.int32, (left_count, right_count), 0) + left_start
    right_idx = lax.broadcasted_iota(jnp.int32, (left_count, right_count), 1) + right_start
    angle_all = (left_idx * right_idx % period).astype(jnp.float32) * (TWO_PI / period)
    return (jnp.cos(angle_all), jnp.sin(angle_all))


def contract(pattern, matrix, values):
    return jnp.einsum(
        pattern, matrix, values, precision=HIGHEST, preferred_element_type=jnp.float32
    )


def forward_spectrum(signal):
    seq_parts = lax.axis_size("seq")
    row_count = signal.shape[0]
    row_share = row_count // seq_parts
    period = 2 * seq_parts * row_count
    spread_in = lax.all_to_all(signal[None], "seq", split_axis=1, concat_axis=0, tiled=True)
    outer_cos, outer_sin = phase_pair(2 * seq_parts, seq_parts, 2 * seq_parts, 0, 0)
    section_re = contract("cp,prw->crw", outer_cos, spread_in)
    section_im = -contract("cp,prw->crw", outer_sin, spread_in)
    twist_cos, twist_sin = phase_pair(
        2 * seq_parts, row_share, period, 0, lax.axis_index("seq") * row_share
    )
    twist_cos = twist_cos[:, :, None]
    twist_sin = twist_sin[:, :, None]
    turned_re = section_re * twist_cos + section_im * twist_sin
    turned_im = section_im * twist_cos - section_re * twist_sin
    inner_cos, inner_sin = phase_pair(row_count, row_count, row_count, 0, 0)
    piece_re = lax.all_to_all(turned_re, "seq", split_axis=0, concat_axis=1, tiled=True)
    piece_im = lax.all_to_all(turned_im, "seq", split_axis=0, concat_axis=1, tiled=True)
    spec_re = contract("dm,cmk->cdk", inner_cos, piece_re) + contract(
        "dm,cmk->cdk", inner_sin, piece_im
    )
    spec_im = contract("dm,cmk->cdk", inner_cos, piece_im) - contract(
        "dm,cmk->cdk", inner_sin, piece_re
    )
    return (spec_re, spec_im)


def time_signal(spec_re, spec_im):
    seq_parts = lax.axis_size("seq")
    row_count = spec_re.shape[1]
    period = 2 * seq_parts * row_count
    inner_cos, inner_sin = phase_pair(row_count, row_count, row_count, 0, 0)
    back_re = contract("md,cdk->cmk", inner_cos, spec_re) - contract(
        "md,cdk->cmk", inner_sin, spec_im
    )
    back_im = contract("md,cdk->cmk", inner_cos, spec_im) + contract(
        "md,cdk->cmk", inner_sin, spec_re
    )
    twist_cos, twist_sin = phase_pair(2, row_count, period, 2 * lax.axis_index("seq"), 0)
    twist_cos = twist_cos[:, :, None]
    twist_sin = twist_sin[:, :, None]
    turned_re = back_re * twist_cos - back_im * twist_sin
    turned_im = back_im * twist_cos + back_re * twist_sin
    outer_cos, outer_sin = phase_pair(seq_parts, 2 * seq_parts, 2 * seq_parts, 0, 0)
    piece_re = lax.all_to_all(turned_re, "seq", split_axis=1, concat_axis=0, tiled=True)
    piece_im = lax.all_to_all(turned_im, "seq", split_axis=1, concat_axis=0, tiled=True)
    summed = contract("pc,crk->prk", outer_cos, piece_re) - contract(
        "pc,crk->prk", outer_sin, piece_im
    )
    returned = summed * (1.0 / period)
    return lax.all_to_all(returned, "seq", split_axis=0, concat_axis=1, tiled=True)[0]


def local(qkv, filt, skip_gain, short_weight, w_out, g_out):
    row_count = qkv.shape[1]
    slab_width = qkv.shape[2]
    tail_rows = passed_along(qkv[:, row_count - 2 :, :], "seq", 1)
    extended = jnp.concatenate([tail_rows, qkv], axis=1)
    short = (
        short_weight[:, 0, None, :] * extended[:, 2:, :]
        + short_weight[:, 1, None, :] * extended[:, 1:-1, :]
        + short_weight[:, 2, None, :] * extended[:, :-2, :]
    )
    query_gate = short[0]
    key_short = short[1]
    value_short = short[2]
    mixed = key_short * value_short
    both_re, both_im = forward_spectrum(jnp.concatenate([mixed, filt], axis=1))
    signal_re = both_re[:, :, :slab_width]
    signal_im = both_im[:, :, :slab_width]
    kernel_re = both_re[:, :, slab_width:]
    kernel_im = both_im[:, :, slab_width:]
    conv_out = time_signal(
        signal_re * kernel_re - signal_im * kernel_im, signal_re * kernel_im + signal_im * kernel_re
    )
    long_out = conv_out + skip_gain * mixed
    gated_out = (query_gate * long_out).astype(jnp.bfloat16)
    projected = jnp.dot(
        lax.all_gather(gated_out, "ch", axis=1, tiled=True),
        w_out,
        preferred_element_type=jnp.float32,
    )
    output = projected.astype(jnp.bfloat16)
    grad_all = lax.all_gather(g_out, "ch", axis=1, tiled=True)
    rows_all = lax.all_to_all(w_out, "ch", split_axis=0, concat_axis=1, tiled=True)
    grad_gated = lax.dot_general(
        grad_all, rows_all, (((1,), (1,)), ((), ())), preferred_element_type=jnp.float32
    )
    grad_long = grad_gated * query_gate
    grad_query = grad_gated * long_out
    grad_re, grad_im = forward_spectrum(grad_long)
    pair_re = jnp.concatenate(
        [kernel_re * grad_re + kernel_im * grad_im, signal_re * grad_re + signal_im * grad_im],
        axis=2,
    )
    pair_im = jnp.concatenate(
        [kernel_re * grad_im - kernel_im * grad_re, signal_re * grad_im - signal_im * grad_re],
        axis=2,
    )
    pair_time = time_signal(pair_re, pair_im)
    grad_mixed = pair_time[:, :slab_width] + skip_gain * grad_long
    token_total = lax.axis_size("seq") * row_count
    grad_filter = pair_time[:, slab_width:] * (1.0 / math.sqrt(token_total))
    grad_short = jnp.stack([grad_query, grad_mixed * value_short, grad_mixed * key_short])
    head_rows = passed_along(grad_short[:, :2, :], "seq", -1)
    extended_grad = jnp.concatenate([grad_short, head_rows], axis=1)
    grad_qkv = (
        short_weight[:, 0, None, :] * extended_grad[:, :-2, :]
        + short_weight[:, 1, None, :] * extended_grad[:, 1:-1, :]
        + short_weight[:, 2, None, :] * extended_grad[:, 2:, :]
    ).astype(jnp.bfloat16)
    return (output, grad_qkv, grad_filter)


def solution(mesh):
    in_specs = (
        P(None, "seq", "ch"),
        P("seq", "ch"),
        P("ch"),
        P(None, None, "ch"),
        P(None, "ch"),
        P("seq", "ch"),
    )
    out_specs = (P("seq", "ch"), P(None, "seq", "ch"), P("seq", "ch"))
    return jax.shard_map(local, mesh=mesh, in_specs=in_specs, out_specs=out_specs, check_vma=False)
```

profile of v0, /device:TPU:1, one launch (start us, length us, event | category | flops | bytes accessed | tf_op | source)
XLA Modules:
  0.0 649.4 jit_solution(5705717059407092852)
XLA Ops:
  0.7 5.0 all-to-all-start.6
  6.4 4.4 collective-permute-start
  10.8 24.7 %all_gather.7 = bf16[128,2048]{1,0:T(8,128)(2,1)S(1)} all-gather(bf16[128,512]{1,0:T(8,128)(2,1)S(1)} %copy-done.18), channel_id=1, replica_groups=mesh['seq'=128,'ch'=4] {'ch'}, dimensions={1}, use_global_device_ids=true | all-gather | bytes 655360 | tf_op jit(solution)/shard_map/all_gather | solution.py:114
  37.1 2.4 copy.51
  42.7 24.8 %all-to-all-start.7 = ((f32[1,128,512]{2,0,1:T(1,128)}), f32[1,128,512]{2,0,1:T(1,128)S(1)}, u32[]{:S(2)}, u32[]{:S(2)}) async-start(f32[1,128,512]{2,0,1:T(1,128)} %copy.52), calls=%async_computation.7 | async-start | bytes 524288 | tf_op jit(solution)/shard_map/all_to_all | solution.py:35
  68.9 21.0 %all-to-all-done.7 = f32[1,128,512]{2,0,1:T(1,128)S(1)} async-done(((f32[1,128,512]{2,0,1:T(1,128)}), f32[1,128,512]{2,0,1:T(1,128)S(1)}, u32[]{:S(2)}, u32[]{:S(2)}) %all-to-all-start.7) | async-done | bytes 262176 | tf_op jit(solution)/shard_map/all_to_all | solution.py:35
  89.9 7.4 %all-to-all-start = ((f32[1,128,1024]{2,0,1:T(1,128)}), f32[1,128,1024]{2,0,1:T(1,128)S(1)}, u32[]{:S(2)}, u32[]{:S(2)}) async-start(f32[1,128,1024]{2,0,1:T(1,128)} %copy.43), calls=%async_computation | async-start | bytes 1048576 | tf_op jit(solution)/shard_map/all_to_all | solution.py:35
  100.9 29.7 %all-to-all-done = f32[1,128,1024]{2,0,1:T(1,128)S(1)} async-done(((f32[1,128,1024]{2,0,1:T(1,128)}), f32[1,128,1024]{2,0,1:T(1,128)S(1)}, u32[]{:S(2)}, u32[]{:S(2)}) %all-to-all-start) | async-done | bytes 524320 | tf_op jit(solution)/shard_map/all_to_all | solution.py:35
  130.6 7.1 %all-to-all-start.8 = ((f32[256,1,512]{2,1,0:T(1,128)}), f32[256,1,512]{2,1,0:T(1,128)S(1)}, u32[]{:S(2)}, u32[]{:S(2)}) async-start(f32[256,1,512]{2,1,0:T(1,128)} %copy.53), calls=%async_computation.8 | async-start | bytes 1048576 | tf_op jit(solution)/shard_map/all_to_all | solution.py:47
  139.1 31.9 %all-to-all-done.8 = f32[256,1,512]{2,1,0:T(1,128)S(1)} async-done(((f32[256,1,512]{2,1,0:T(1,128)}), f32[256,1,512]{2,1,0:T(1,128)S(1)}, u32[]{:S(2)}, u32[]{:S(2)}) %all-to-all-start.8) | async-done | bytes 524320 | tf_op jit(solution)/shard_map/all_to_all | solution.py:47
  170.9 7.6 %all-to-all-start.9 = ((f32[256,1,512]{2,1,0:T(1,128)}), f32[256,1,512]{2,1,0:T(1,128)S(1)}, u32[]{:S(2)}, u32[]{:S(2)}) async-start(f32[256,1,512]{2,1,0:T(1,128)} %copy.55), calls=%async_computation.9 | async-start | bytes 1048576 | tf_op jit(solution)/shard_map/all_to_all | solution.py:48
  183.8 27.9 %all-to-all-done.9 = f32[256,1,512]{2,1,0:T(1,128)S(1)} async-done(((f32[256,1,512]{2,1,0:T(1,128)}), f32[256,1,512]{2,1,0:T(1,128)S(1)}, u32[]{:S(2)}, u32[]{:S(2)}) %all-to-all-start.9) | async-done | bytes 524320 | tf_op jit(solution)/shard_map/all_to_all | solution.py:48
  211.7 7.6 %all-to-all-start.1 = ((f32[256,1,1024]{2,1,0:T(1,128)}), f32[256,1,1024]{2,1,0:T(1,128)}, u32[]{:S(2)}, u32[]{:S(2)}) async-start(f32[256,1,1024]{2,1,0:T(1,128)} %copy.44), calls=%async_computation.1 | async-start | bytes 2097152 | tf_op jit(solution)/shard_map/all_to_all | solution.py:47
  221.4 51.9 %all-to-all-done.1 = f32[256,1,1024]{2,1,0:T(1,128)} async-done(((f32[256,1,1024]{2,1,0:T(1,128)}), f32[256,1,1024]{2,1,0:T(1,128)}, u32[]{:S(2)}, u32[]{:S(2)}) %all-to-all-start.1) | async-done | bytes 1048608 | tf_op jit(solution)/shard_map/all_to_all | solution.py:47
  273.4 8.8 %all-to-all-start.2 = ((f32[256,1,1024]{2,1,0:T(1,128)}), f32[256,1,1024]{2,1,0:T(1,128)S(1)}, u32[]{:S(2)}, u32[]{:S(2)}) async-start(f32[256,1,1024]{2,1,0:T(1,128)} %copy.46), calls=%async_computation.2 | async-start | bytes 2097152 | tf_op jit(solution)/shard_map/all_to_all | solution.py:48
  291.8 44.7 %all-to-all-done.2 = f32[256,1,1024]{2,1,0:T(1,128)S(1)} async-done(((f32[256,1,1024]{2,1,0:T(1,128)}), f32[256,1,1024]{2,1,0:T(1,128)S(1)}, u32[]{:S(2)}, u32[]{:S(2)}) %all-to-all-start.2) | async-done | bytes 1048608 | tf_op jit(solution)/shard_map/all_to_all | solution.py:48
  337.5 2.3 copy.47
  352.0 9.4 %all-to-all-start.3 = ((f32[2,128,512]{2,0,1:T(2,128)}), f32[2,128,512]{2,0,1:T(2,128)}, u32[]{:S(2)}, u32[]{:S(2)}) async-start(f32[2,128,512]{2,0,1:T(2,128)} %copy.48), calls=%async_computation.3 | async-start | bytes 1048576 | tf_op jit(solution)/shard_map/all_to_all | solution.py:75
  365.1 2.4 add_bitcast_fusion
  369.7 24.3 %all-to-all-done.3 = f32[2,128,512]{2,0,1:T(2,128)} async-done(((f32[2,128,512]{2,0,1:T(2,128)}), f32[2,128,512]{2,0,1:T(2,128)}, u32[]{:S(2)}, u32[]{:S(2)}) %all-to-all-start.3) | async-done | bytes 524320 | tf_op jit(solution)/shard_map/all_to_all | solution.py:75
  394.1 7.1 %all-to-all-start.10 = ((f32[2,128,1024]{2,0,1:T(2,128)}), f32[2,128,1024]{2,0,1:T(2,128)S(1)}, u32[]{:S(2)}, u32[]{:S(2)}) async-start(f32[2,128,1024]{2,0,1:T(2,128)} %copy.57), calls=%async_computation.10 | async-start | bytes 2097152 | tf_op jit(solution)/shard_map/all_to_all | solution.py:75
  402.5 53.1 %all-to-all-done.10 = f32[2,128,1024]{2,0,1:T(2,128)S(1)} async-done(((f32[2,128,1024]{2,0,1:T(2,128)}), f32[2,128,1024]{2,0,1:T(2,128)S(1)}, u32[]{:S(2)}, u32[]{:S(2)}) %all-to-all-start.10) | async-done | bytes 1048608 | tf_op jit(solution)/shard_map/all_to_all | solution.py:75
  455.6 8.4 %all-to-all-start.11 = ((f32[2,128,1024]{2,0,1:T(2,128)}), f32[2,128,1024]{2,0,1:T(2,128)S(1)}, u32[]{:S(2)}, u32[]{:S(2)}) async-start(f32[2,128,1024]{2,0,1:T(2,128)} %copy.58), calls=%async_computation.11 | async-start | bytes 2097152 | tf_op jit(solution)/shard_map/all_to_all | solution.py:76
  465.0 53.4 %all-to-all-done.11 = f32[2,128,1024]{2,0,1:T(2,128)S(1)} async-done(((f32[2,128,1024]{2,0,1:T(2,128)}), f32[2,128,1024]{2,0,1:T(2,128)S(1)}, u32[]{:S(2)}, u32[]{:S(2)}) %all-to-all-start.11) | async-done | bytes 1048608 | tf_op jit(solution)/shard_map/all_to_all | solution.py:76
  518.4 8.7 %all-to-all-start.4 = ((f32[2,128,512]{2,0,1:T(2,128)}), f32[2,128,512]{2,0,1:T(2,128)S(1)}, u32[]{:S(2)}, u32[]{:S(2)}) async-start(f32[2,128,512]{2,0,1:T(2,128)} %copy.49), calls=%async_computation.4 | async-start | bytes 1048576 | tf_op jit(solution)/shard_map/all_to_all | solution.py:76
  534.3 25.9 %all-to-all-done.4 = f32[2,128,512]{2,0,1:T(2,128)S(1)} async-done(((f32[2,128,512]{2,0,1:T(2,128)}), f32[2,128,512]{2,0,1:T(2,128)S(1)}, u32[]{:S(2)}, u32[]{:S(2)}) %all-to-all-start.4) | async-done | bytes 524320 | tf_op jit(solution)/shard_map/all_to_all | solution.py:76
  560.2 7.1 %all-to-all-start.12 = ((f32[128,1,1024]{2,1,0:T(1,128)}), f32[128,1,1024]{2,1,0:T(1,128)S(1)}, u32[]{:S(2)}, u32[]{:S(2)}) async-start(f32[128,1,1024]{2,1,0:T(1,128)} %copy.59), calls=%async_computation.12 | async-start | bytes 1048576 | tf_op jit(solution)/shard_map/all_to_all | solution.py:81
  572.0 28.5 %all-to-all-done.12 = f32[128,1,1024]{2,1,0:T(1,128)S(1)} async-done(((f32[128,1,1024]{2,1,0:T(1,128)}), f32[128,1,1024]{2,1,0:T(1,128)S(1)}, u32[]{:S(2)}, u32[]{:S(2)}) %all-to-all-start.12) | async-done | bytes 524320 | tf_op jit(solution)/shard_map/all_to_all | solution.py:81
  600.5 7.1 %all-to-all-start.5 = ((f32[128,1,512]{2,1,0:T(1,128)}), f32[128,1,512]{2,1,0:T(1,128)S(1)}, u32[]{:S(2)}, u32[]{:S(2)}) async-start(f32[128,1,512]{2,1,0:T(1,128)} %copy.50), calls=%async_computation.5 | async-start | bytes 524288 | tf_op jit(solution)/shard_map/all_to_all | solution.py:81
  607.8 22.3 %all-to-all-done.5 = f32[128,1,512]{2,1,0:T(1,128)S(1)} async-done(((f32[128,1,512]{2,1,0:T(1,128)}), f32[128,1,512]{2,1,0:T(1,128)S(1)}, u32[]{:S(2)}, u32[]{:S(2)}) %all-to-all-start.5) | async-done | bytes 262176 | tf_op jit(solution)/shard_map/all_to_all | solution.py:81
  631.1 4.3 collective-permute-start.1
  635.4 11.6 %all_gather.6 = bf16[128,2048]{1,0:T(8,128)(2,1)S(1)} all-gather(bf16[128,512]{1,0:T(8,128)(2,1)S(1)} %get-tuple-element.19), channel_id=1, replica_groups=mesh['seq'=128,'ch'=4] {'ch'}, dimensions={1}, use_global_device_ids=true | all-gather | bytes 655360 | tf_op jit(solution)/shard_map/all_gather | solution.py:109
  (106 shorter events, 65.2 us)
Async XLA Ops:
  0.6 10.1 %copy-start.19 = (f32[3,3,512]{2,1,0:T(4,128)S(1)}, f32[3,3,512]{2,1,0:T(4,128)}, u32[]{:S(2)}) copy-start(f32[3,3,512]{2,1,0:T(4,128)} %param.9) | copy-start | bytes 55300
  0.6 10.2 %copy-start.18 = (bf16[128,512]{1,0:T(8,128)(2,1)S(1)}, bf16[128,512]{1,0:T(8,128)(2,1)}, u32[]{:S(2)}) copy-start(bf16[128,512]{1,0:T(8,128)(2,1)} %param.11) | copy-start | bytes 393220
  0.7 36.4 %all-to-all-start.6 = ((bf16[4,512,512]{2,1,0:T(8,128)(2,1)}), bf16[4,512,512]{2,1,0:T(8,128)(2,1)S(1)}, u32[]{:S(2)}, u32[]{:S(2)}) async-start(bf16[4,512,512]{2,1,0:T(8,128)(2,1)} %bitcast.200), calls=%async_computation.6 | async-start | bytes 4194304 | tf_op jit(solution)/shard_map/all_to_all | solution.py:115
  6.4 29.1 %collective-permute-start = (bf16[3,2,512]{2,1,0:T(2,128)(2,1)S(1)}, bf16[3,2,512]{2,1,0:T(2,128)(2,1)S(1)}, u32[]{:S(2)}, u32[]{:S(2)}) collective-permute-start(bf16[3,2,512]{2,1,0:T(2,128)(2,1)S(1)} %slice.59), channel_id=1, source_target_pairs={{0,4},{4,8},{8,12},{12,16},{16,20},{20,24},{24,28},{28,32},{32,36}... | collective-permute-start | bytes 18440 | tf_op jit(solution)/shard_map/ppermute | solution.py:14
  39.5 28.0 %copy-start.17 = (f32[128,512]{1,0:T(8,128)S(1)}, f32[128,512]{1,0:T(8,128)}, u32[]{:S(2)}) copy-start(f32[128,512]{1,0:T(8,128)} %param.7) | copy-start | bytes 786436
  41.6 27.3 %copy-start.8 = (f32[128,512]{1,0:T(8,128)}, f32[128,512]{1,0:T(8,128)S(1)}, u32[]{:S(2)}) copy-start(f32[128,512]{1,0:T(8,128)S(1)} %fusion.230) | copy-start | bytes 786436
  41.7 48.2 %copy-start.6 = (f32[128,512]{1,0:T(8,128)}, f32[128,512]{1,0:T(8,128)S(1)}, u32[]{:S(2)}) copy-start(f32[128,512]{1,0:T(8,128)S(1)} %get-tuple-element.22) | copy-start | bytes 786436
  42.7 47.2 %all-to-all-start.7 = ((f32[1,128,512]{2,0,1:T(1,128)}), f32[1,128,512]{2,0,1:T(1,128)S(1)}, u32[]{:S(2)}, u32[]{:S(2)}) async-start(f32[1,128,512]{2,0,1:T(1,128)} %copy.52), calls=%async_computation.7 | async-start | bytes 524288 | tf_op jit(solution)/shard_map/all_to_all | solution.py:35
  89.9 40.7 %all-to-all-start = ((f32[1,128,1024]{2,0,1:T(1,128)}), f32[1,128,1024]{2,0,1:T(1,128)S(1)}, u32[]{:S(2)}, u32[]{:S(2)}) async-start(f32[1,128,1024]{2,0,1:T(1,128)} %copy.43), calls=%async_computation | async-start | bytes 1048576 | tf_op jit(solution)/shard_map/all_to_all | solution.py:35
  130.6 40.3 %all-to-all-start.8 = ((f32[256,1,512]{2,1,0:T(1,128)}), f32[256,1,512]{2,1,0:T(1,128)S(1)}, u32[]{:S(2)}, u32[]{:S(2)}) async-start(f32[256,1,512]{2,1,0:T(1,128)} %copy.53), calls=%async_computation.8 | async-start | bytes 1048576 | tf_op jit(solution)/shard_map/all_to_all | solution.py:47
  170.9 10.8 %copy-start.10 = (f32[256,1,512]{2,1,0:T(1,128)}, f32[256,1,512]{2,1,0:T(1,128)S(1)}, u32[]{:S(2)}) copy-start(f32[256,1,512]{2,1,0:T(1,128)S(1)} %all-to-all-done.8) | copy-start | bytes 1572868
  170.9 40.8 %all-to-all-start.9 = ((f32[256,1,512]{2,1,0:T(1,128)}), f32[256,1,512]{2,1,0:T(1,128)S(1)}, u32[]{:S(2)}, u32[]{:S(2)}) async-start(f32[256,1,512]{2,1,0:T(1,128)} %copy.55), calls=%async_computation.9 | async-start | bytes 1048576 | tf_op jit(solution)/shard_map/all_to_all | solution.py:48
  211.7 9.7 %copy-start.12 = (f32[256,1,512]{2,1,0:T(1,128)}, f32[256,1,512]{2,1,0:T(1,128)S(1)}, u32[]{:S(2)}) copy-start(f32[256,1,512]{2,1,0:T(1,128)S(1)} %all-to-all-done.9) | copy-start | bytes 1572868
  211.7 61.7 %all-to-all-start.1 = ((f32[256,1,1024]{2,1,0:T(1,128)}), f32[256,1,1024]{2,1,0:T(1,128)}, u32[]{:S(2)}, u32[]{:S(2)}) async-start(f32[256,1,1024]{2,1,0:T(1,128)} %copy.44), calls=%async_computation.1 | async-start | bytes 2097152 | tf_op jit(solution)/shard_map/all_to_all | solution.py:47
  219.3 63.0 %copy-start.11 = (f32[256,1,512]{2,1,0:T(1,128)S(1)}, f32[256,1,512]{2,1,0:T(1,128)}, u32[]{:S(2)}) copy-start(f32[256,1,512]{2,1,0:T(1,128)} %copy-done.10) | copy-start | bytes 1572868
  273.4 9.4 %copy-start.13 = (f32[256,1,512]{2,1,0:T(1,128)S(1)}, f32[256,1,512]{2,1,0:T(1,128)}, u32[]{:S(2)}) copy-start(f32[256,1,512]{2,1,0:T(1,128)} %copy-done.12) | copy-start | bytes 1572868
  273.4 63.1 %all-to-all-start.2 = ((f32[256,1,1024]{2,1,0:T(1,128)}), f32[256,1,1024]{2,1,0:T(1,128)S(1)}, u32[]{:S(2)}, u32[]{:S(2)}) async-start(f32[256,1,1024]{2,1,0:T(1,128)} %copy.46), calls=%async_computation.2 | async-start | bytes 2097152 | tf_op jit(solution)/shard_map/all_to_all | solution.py:48
  342.4 1.3 copy-start.15
  348.1 13.3 %copy-start.1 = (f32[2,128,512]{1,2,0:T(8,128)S(1)}, f32[2,128,512]{1,2,0:T(8,128)}, u32[]{:S(2)}) copy-start(f32[2,128,512]{1,2,0:T(8,128)} %get-tuple-element.8) | copy-start | bytes 1572868
  352.0 42.1 %all-to-all-start.3 = ((f32[2,128,512]{2,0,1:T(2,128)}), f32[2,128,512]{2,0,1:T(2,128)}, u32[]{:S(2)}, u32[]{:S(2)}) async-start(f32[2,128,512]{2,0,1:T(2,128)} %copy.48), calls=%async_computation.3 | async-start | bytes 1048576 | tf_op jit(solution)/shard_map/all_to_all | solution.py:75
  394.1 61.5 %all-to-all-start.10 = ((f32[2,128,1024]{2,0,1:T(2,128)}), f32[2,128,1024]{2,0,1:T(2,128)S(1)}, u32[]{:S(2)}, u32[]{:S(2)}) async-start(f32[2,128,1024]{2,0,1:T(2,128)} %copy.57), calls=%async_computation.10 | async-start | bytes 2097152 | tf_op jit(solution)/shard_map/all_to_all | solution.py:75
  401.2 62.8 %copy-start.14 = (f32[2,128,512]{1,2,0:T(8,128)S(1)}, f32[2,128,512]{1,2,0:T(8,128)}, u32[]{:S(2)}) copy-start(f32[2,128,512]{1,2,0:T(8,128)} %get-tuple-element.17) | copy-start | bytes 1572868
  455.6 62.8 %all-to-all-start.11 = ((f32[2,128,1024]{2,0,1:T(2,128)}), f32[2,128,1024]{2,0,1:T(2,128)S(1)}, u32[]{:S(2)}, u32[]{:S(2)}) async-start(f32[2,128,1024]{2,0,1:T(2,128)} %copy.58), calls=%async_computation.11 | async-start | bytes 2097152 | tf_op jit(solution)/shard_map/all_to_all | solution.py:76
  518.4 41.8 %all-to-all-start.4 = ((f32[2,128,512]{2,0,1:T(2,128)}), f32[2,128,512]{2,0,1:T(2,128)S(1)}, u32[]{:S(2)}, u32[]{:S(2)}) async-start(f32[2,128,512]{2,0,1:T(2,128)} %copy.49), calls=%async_computation.4 | async-start | bytes 1048576 | tf_op jit(solution)/shard_map/all_to_all | solution.py:76
  528.8 1.7 copy-start.4
  560.2 40.3 %all-to-all-start.12 = ((f32[128,1,1024]{2,1,0:T(1,128)}), f32[128,1,1024]{2,1,0:T(1,128)S(1)}, u32[]{:S(2)}, u32[]{:S(2)}) async-start(f32[128,1,1024]{2,1,0:T(1,128)} %copy.59), calls=%async_computation.12 | async-start | bytes 1048576 | tf_op jit(solution)/shard_map/all_to_all | solution.py:81
  569.1 61.0 %copy-start.7 = (f32[128,512]{1,0:T(8,128)S(1)}, f32[128,512]{1,0:T(8,128)}, u32[]{:S(2)}) copy-start(f32[128,512]{1,0:T(8,128)} %copy-done.6) | copy-start | bytes 786436
  569.1 61.0 %copy-start.9 = (f32[128,512]{1,0:T(8,128)S(1)}, f32[128,512]{1,0:T(8,128)}, u32[]{:S(2)}) copy-start(f32[128,512]{1,0:T(8,128)} %copy-done.8) | copy-start | bytes 786436
  569.1 61.0 %copy-start.20 = (f32[512]{0:T(512)S(1)}, f32[512]{0:T(512)}, u32[]{:S(2)}) copy-start(f32[512]{0:T(512)} %param.8) | copy-start | bytes 6148
  600.5 29.5 %all-to-all-start.5 = ((f32[128,1,512]{2,1,0:T(1,128)}), f32[128,1,512]{2,1,0:T(1,128)S(1)}, u32[]{:S(2)}, u32[]{:S(2)}) async-start(f32[128,1,512]{2,1,0:T(1,128)} %copy.50), calls=%async_computation.5 | async-start | bytes 524288 | tf_op jit(solution)/shard_map/all_to_all | solution.py:81
  631.0 16.0 %copy-start = (bf16[2048,512]{1,0:T(8,128)(2,1)S(1)}, bf16[2048,512]{1,0:T(8,128)(2,1)}, u32[]{:S(2)}) copy-start(bf16[2048,512]{1,0:T(8,128)(2,1)} %param.10) | copy-start | bytes 6291460
  631.1 17.0 %collective-permute-start.1 = (f32[3,2,512]{2,1,0:T(2,128)S(1)}, f32[3,2,512]{2,1,0:T(2,128)S(1)}, u32[]{:S(2)}, u32[]{:S(2)}) collective-permute-start(f32[3,2,512]{2,1,0:T(2,128)S(1)} %slice.85), channel_id=1, source_target_pairs={{4,0},{8,4},{12,8},{16,12},{20,16},{24,20},{28,24},{32,28},{36,32}... | collective-permute-start | bytes 36872 | tf_op jit(solution)/shard_map/ppermute | solution.py:14
  (4 other events, 4.8 us)
where the time goes:
time: 659 us; the launch traced here: 649 us
  waiting for transfers between devices  415 us (63%)
  starting transfers between devices  125 us (19%)
  blocking collectives  36.3 us (6%)
  matrix products  35.1 us (5%)
  local copies, waits for them, and re-layouts  33.2 us (5%)
    all_to_all x2, waiting for transfers between devices, forward_spectrum(): lax.all_to_all(turned_re, 'seq', split_axis=0, concat_axis=1, tiled=True)  83.8 us
    all_to_all x2, waiting for transfers between devices, time_signal(): lax.all_to_all(turned_im, 'seq', split_axis=1, concat_axis=0, tiled=True)  79.3 us
    all_to_all x2, waiting for transfers between devices, time_signal(): lax.all_to_all(turned_re, 'seq', split_axis=1, concat_axis=0, tiled=True)  77.4 us
    all_to_all x2, waiting for transfers between devices, forward_spectrum(): lax.all_to_all(turned_im, 'seq', split_axis=0, concat_axis=1, tiled=True)  72.7 us
    all_to_all x2, waiting for transfers between devices, time_signal(): lax.all_to_all(returned, 'seq', split_axis=0, concat_axis=1, tiled=True)[0]  50.8 us
    all_to_all x2, waiting for transfers between devices, forward_spectrum(): lax.all_to_all(signal[None], 'seq', split_axis=1, concat_axis=0, tiled=True)  50.7 us
    all_to_all x2, starting transfers between devices, forward_spectrum(): lax.all_to_all(signal[None], 'seq', split_axis=1, concat_axis=0, tiled=True)  32.2 us
    dot_general x24, matrix products, contract(): jnp.einsum(pattern, matrix, values, precision=HIGHEST, preferred_element_...  32 us
  transfers between devices with their start and end apart: 15, of which 12 were waited for; matrix products, arithmetic and copies ran while one was open for 8% of the time, Pallas kernels for 0%

commit v1 on v0

--- a/solution.py
+++ b/solution.py
@@ -111,7 +111,8 @@
         preferred_element_type=jnp.float32,
     )
     output = projected.astype(jnp.bfloat16)
-    grad_all = lax.all_gather(g_out, "ch", axis=1, tiled=True)
+    outgoing = jnp.stack([g_out] * lax.axis_size("ch"))
+    grad_all = jnp.concatenate(lax.all_to_all(outgoing, "ch", 0, 0), axis=1)
     rows_all = lax.all_to_all(w_out, "ch", split_axis=0, concat_axis=1, tiled=True)
     grad_gated = lax.dot_general(
         grad_all, rows_all, (((1,), (1,)), ((), ())), preferred_element_type=jnp.float32

time: 659 us -> 658 us (level)
  blocking collectives: 36.3 us -> 23.2 us
  waiting for transfers between devices: 415 us -> 425 us
    all_gather x1 -> x0, blocking collectives: 24.7 us -> none  [local(): grad_all = lax.all_gather(g_out, 'ch', axis=1, tiled=True)]
    all_to_all x0 -> x1, blocking collectives: none -> 11.6 us  [local(): grad_all = jnp.concatenate(lax.all_to_all(outgoing, 'ch', 0, 0), axis=1)]
    all_to_all x1, waiting for transfers between devices: 0.01 us -> 10.3 us  [local(): lax.all_to_all(w_out, 'ch', split_axis=0, concat_axis=1, tiled=True)]
  transfers between devices with their start and end apart: 15 -> 15, of which waited for: 12 -> 14; matrix products, arithmetic and copies ran while one was open for 8% -> 8% of each run, Pallas kernels for 0% -> 0%
where the time goes in v1:
time: 658 us; the launch traced here: 648 us
  waiting for transfers between devices  425 us (65%)
  starting transfers between devices  129 us (20%)
  matrix products  33.8 us (5%)
  local copies, waits for them, and re-layouts  31.5 us (5%)
  blocking collectives  23.2 us (4%)
    all_to_all x2, waiting for transfers between devices, forward_spectrum(): lax.all_to_all(turned_re, 'seq', split_axis=0, concat_axis=1, tiled=True)  83.8 us
    all_to_all x2, waiting for transfers between devices, time_signal(): lax.all_to_all(turned_im, 'seq', split_axis=1, concat_axis=0, tiled=True)  79.3 us
    all_to_all x2, waiting for transfers between devices, time_signal(): lax.all_to_all(turned_re, 'seq', split_axis=1, concat_axis=0, tiled=True)  77.4 us
    all_to_all x2, waiting for transfers between devices, forward_spectrum(): lax.all_to_all(turned_im, 'seq', split_axis=0, concat_axis=1, tiled=True)  72.4 us
    all_to_all x2, waiting for transfers between devices, time_signal(): lax.all_to_all(returned, 'seq', split_axis=0, concat_axis=1, tiled=True)[0]  50.8 us
    all_to_all x2, waiting for transfers between devices, forward_spectrum(): lax.all_to_all(signal[None], 'seq', split_axis=1, concat_axis=0, tiled=True)  50.7 us
    all_to_all x2, starting transfers between devices, forward_spectrum(): lax.all_to_all(signal[None], 'seq', split_axis=1, concat_axis=0, tiled=True)  35 us
    dot_general x24, matrix products, contract(): jnp.einsum(pattern, matrix, values, precision=HIGHEST, preferred_element_...  31.9 us
  transfers between devices with their start and end apart: 15, of which 14 were waited for; matrix products, arithmetic and copies ran while one was open for 8% of the time, Pallas kernels for 0%

profile of v1, /device:TPU:1, one launch (start us, length us, event | category | flops | bytes accessed | tf_op | source)
XLA Modules:
  0.0 648.1 jit_solution(13509799022857387967)
XLA Ops:
  1.6 11.6 %all_to_all.189 = bf16[4,128,512]{2,1,0:T(8,128)(2,1)S(1)} all-to-all(bf16[4,128,512]{2,1,0:T(8,128)(2,1)S(1)} %stack.19), channel_id=1, replica_groups=mesh['seq'=128,'ch'=4] {'ch'}, dimensions={0} | all-to-all | bytes 1048576 | tf_op jit(solution)/shard_map/all_to_all | solution.py:115
  13.1 3.7 all-to-all-start.7
  17.6 6.9 %collective-permute-start = (bf16[3,2,512]{2,1,0:T(2,128)(2,1)S(1)}, bf16[3,2,512]{2,1,0:T(2,128)(2,1)S(1)}, u32[]{:S(2)}, u32[]{:S(2)}) collective-permute-start(bf16[3,2,512]{2,1,0:T(2,128)(2,1)S(1)} %slice.59), channel_id=1, source_target_pairs={{0,4},{4,8},{8,12},{12,16},{16,20},{20,24},{24,28},{28,32},{32,36}... | collective-permute-start | bytes 18440 | tf_op jit(solution)/shard_map/ppermute | solution.py:14
  26.9 10.3 %all-to-all-done.7 = bf16[4,512,512]{2,1,0:T(8,128)(2,1)S(1)} async-done(((bf16[4,512,512]{2,1,0:T(8,128)(2,1)}), bf16[4,512,512]{2,1,0:T(8,128)(2,1)S(1)}, u32[]{:S(2)}, u32[]{:S(2)}) %all-to-all-start.7) | async-done | bytes 2097184 | tf_op jit(solution)/shard_map/all_to_all | solution.py:116
  39.8 27.7 %all-to-all-start.8 = ((f32[1,128,512]{2,0,1:T(1,128)}), f32[1,128,512]{2,0,1:T(1,128)S(1)}, u32[]{:S(2)}, u32[]{:S(2)}) async-start(f32[1,128,512]{2,0,1:T(1,128)} %copy.41), calls=%async_computation.8 | async-start | bytes 524288 | tf_op jit(solution)/shard_map/all_to_all | solution.py:35
  68.9 21.0 %all-to-all-done.8 = f32[1,128,512]{2,0,1:T(1,128)S(1)} async-done(((f32[1,128,512]{2,0,1:T(1,128)}), f32[1,128,512]{2,0,1:T(1,128)S(1)}, u32[]{:S(2)}, u32[]{:S(2)}) %all-to-all-start.8) | async-done | bytes 262176 | tf_op jit(solution)/shard_map/all_to_all | solution.py:35
  89.9 7.4 %all-to-all-start = ((f32[1,128,1024]{2,0,1:T(1,128)}), f32[1,128,1024]{2,0,1:T(1,128)S(1)}, u32[]{:S(2)}, u32[]{:S(2)}) async-start(f32[1,128,1024]{2,0,1:T(1,128)} %copy.33), calls=%async_computation | async-start | bytes 1048576 | tf_op jit(solution)/shard_map/all_to_all | solution.py:35
  100.9 29.7 %all-to-all-done = f32[1,128,1024]{2,0,1:T(1,128)S(1)} async-done(((f32[1,128,1024]{2,0,1:T(1,128)}), f32[1,128,1024]{2,0,1:T(1,128)S(1)}, u32[]{:S(2)}, u32[]{:S(2)}) %all-to-all-start) | async-done | bytes 524320 | tf_op jit(solution)/shard_map/all_to_all | solution.py:35
  130.6 7.1 %all-to-all-start.9 = ((f32[256,1,512]{2,1,0:T(1,128)}), f32[256,1,512]{2,1,0:T(1,128)S(1)}, u32[]{:S(2)}, u32[]{:S(2)}) async-start(f32[256,1,512]{2,1,0:T(1,128)} %copy.42), calls=%async_computation.9 | async-start | bytes 1048576 | tf_op jit(solution)/shard_map/all_to_all | solution.py:47
  139.1 31.9 %all-to-all-done.9 = f32[256,1,512]{2,1,0:T(1,128)S(1)} async-done(((f32[256,1,512]{2,1,0:T(1,128)}), f32[256,1,512]{2,1,0:T(1,128)S(1)}, u32[]{:S(2)}, u32[]{:S(2)}) %all-to-all-start.9) | async-done | bytes 524320 | tf_op jit(solution)/shard_map/all_to_all | solution.py:47
  170.9 7.1 %all-to-all-start.10 = ((f32[256,1,512]{2,1,0:T(1,128)}), f32[256,1,512]{2,1,0:T(1,128)S(1)}, u32[]{:S(2)}, u32[]{:S(2)}) async-start(f32[256,1,512]{2,1,0:T(1,128)} %copy.44), calls=%async_computation.10 | async-start | bytes 1048576 | tf_op jit(solution)/shard_map/all_to_all | solution.py:48
  183.3 27.9 %all-to-all-done.10 = f32[256,1,512]{2,1,0:T(1,128)S(1)} async-done(((f32[256,1,512]{2,1,0:T(1,128)}), f32[256,1,512]{2,1,0:T(1,128)S(1)}, u32[]{:S(2)}, u32[]{:S(2)}) %all-to-all-start.10) | async-done | bytes 524320 | tf_op jit(solution)/shard_map/all_to_all | solution.py:48
  211.3 7.6 %all-to-all-start.1 = ((f32[256,1,1024]{2,1,0:T(1,128)}), f32[256,1,1024]{2,1,0:T(1,128)}, u32[]{:S(2)}, u32[]{:S(2)}) async-start(f32[256,1,1024]{2,1,0:T(1,128)} %copy.34), calls=%async_computation.1 | async-start | bytes 2097152 | tf_op jit(solution)/shard_map/all_to_all | solution.py:47
  221.0 52.0 %all-to-all-done.1 = f32[256,1,1024]{2,1,0:T(1,128)} async-done(((f32[256,1,1024]{2,1,0:T(1,128)}), f32[256,1,1024]{2,1,0:T(1,128)}, u32[]{:S(2)}, u32[]{:S(2)}) %all-to-all-start.1) | async-done | bytes 1048608 | tf_op jit(solution)/shard_map/all_to_all | solution.py:47
  272.9 9.0 %all-to-all-start.2 = ((f32[256,1,1024]{2,1,0:T(1,128)}), f32[256,1,1024]{2,1,0:T(1,128)}, u32[]{:S(2)}, u32[]{:S(2)}) async-start(f32[256,1,1024]{2,1,0:T(1,128)} %copy.36), calls=%async_computation.2 | async-start | bytes 2097152 | tf_op jit(solution)/shard_map/all_to_all | solution.py:48
  291.5 44.5 %all-to-all-done.2 = f32[256,1,1024]{2,1,0:T(1,128)} async-done(((f32[256,1,1024]{2,1,0:T(1,128)}), f32[256,1,1024]{2,1,0:T(1,128)}, u32[]{:S(2)}, u32[]{:S(2)}) %all-to-all-start.2) | async-done | bytes 1048608 | tf_op jit(solution)/shard_map/all_to_all | solution.py:48
  336.0 2.5 copy.37
  350.6 9.3 %all-to-all-start.3 = ((f32[2,128,512]{2,0,1:T(2,128)}), f32[2,128,512]{2,0,1:T(2,128)}, u32[]{:S(2)}, u32[]{:S(2)}) async-start(f32[2,128,512]{2,0,1:T(2,128)} %copy.38), calls=%async_computation.3 | async-start | bytes 1048576 | tf_op jit(solution)/shard_map/all_to_all | solution.py:75
  363.6 2.3 add_bitcast_fusion
  368.2 24.4 %all-to-all-done.3 = f32[2,128,512]{2,0,1:T(2,128)} async-done(((f32[2,128,512]{2,0,1:T(2,128)}), f32[2,128,512]{2,0,1:T(2,128)}, u32[]{:S(2)}, u32[]{:S(2)}) %all-to-all-start.3) | async-done | bytes 524320 | tf_op jit(solution)/shard_map/all_to_all | solution.py:75
  392.5 7.1 %all-to-all-start.11 = ((f32[2,128,1024]{2,0,1:T(2,128)}), f32[2,128,1024]{2,0,1:T(2,128)S(1)}, u32[]{:S(2)}, u32[]{:S(2)}) async-start(f32[2,128,1024]{2,0,1:T(2,128)} %copy.46), calls=%async_computation.11 | async-start | bytes 2097152 | tf_op jit(solution)/shard_map/all_to_all | solution.py:75
  401.0 53.1 %all-to-all-done.11 = f32[2,128,1024]{2,0,1:T(2,128)S(1)} async-done(((f32[2,128,1024]{2,0,1:T(2,128)}), f32[2,128,1024]{2,0,1:T(2,128)S(1)}, u32[]{:S(2)}, u32[]{:S(2)}) %all-to-all-start.11) | async-done | bytes 1048608 | tf_op jit(solution)/shard_map/all_to_all | solution.py:75
  454.0 8.4 %all-to-all-start.12 = ((f32[2,128,1024]{2,0,1:T(2,128)}), f32[2,128,1024]{2,0,1:T(2,128)S(1)}, u32[]{:S(2)}, u32[]{:S(2)}) async-start(f32[2,128,1024]{2,0,1:T(2,128)} %copy.47), calls=%async_computation.12 | async-start | bytes 2097152 | tf_op jit(solution)/shard_map/all_to_all | solution.py:76
  463.4 53.4 %all-to-all-done.12 = f32[2,128,1024]{2,0,1:T(2,128)S(1)} async-done(((f32[2,128,1024]{2,0,1:T(2,128)}), f32[2,128,1024]{2,0,1:T(2,128)S(1)}, u32[]{:S(2)}, u32[]{:S(2)}) %all-to-all-start.12) | async-done | bytes 1048608 | tf_op jit(solution)/shard_map/all_to_all | solution.py:76
  516.8 8.8 %all-to-all-start.4 = ((f32[2,128,512]{2,0,1:T(2,128)}), f32[2,128,512]{2,0,1:T(2,128)S(1)}, u32[]{:S(2)}, u32[]{:S(2)}) async-start(f32[2,128,512]{2,0,1:T(2,128)} %copy.39), calls=%async_computation.4 | async-start | bytes 1048576 | tf_op jit(solution)/shard_map/all_to_all | solution.py:76
  532.8 25.9 %all-to-all-done.4 = f32[2,128,512]{2,0,1:T(2,128)S(1)} async-done(((f32[2,128,512]{2,0,1:T(2,128)}), f32[2,128,512]{2,0,1:T(2,128)S(1)}, u32[]{:S(2)}, u32[]{:S(2)}) %all-to-all-start.4) | async-done | bytes 524320 | tf_op jit(solution)/shard_map/all_to_all | solution.py:76
  558.7 7.1 %all-to-all-start.13 = ((f32[128,1,1024]{2,1,0:T(1,128)}), f32[128,1,1024]{2,1,0:T(1,128)S(1)}, u32[]{:S(2)}, u32[]{:S(2)}) async-start(f32[128,1,1024]{2,1,0:T(1,128)} %copy.48), calls=%async_computation.13 | async-start | bytes 1048576 | tf_op jit(solution)/shard_map/all_to_all | solution.py:81
  570.5 28.5 %all-to-all-done.13 = f32[128,1,1024]{2,1,0:T(1,128)S(1)} async-done(((f32[128,1,1024]{2,1,0:T(1,128)}), f32[128,1,1024]{2,1,0:T(1,128)S(1)}, u32[]{:S(2)}, u32[]{:S(2)}) %all-to-all-start.13) | async-done | bytes 524320 | tf_op jit(solution)/shard_map/all_to_all | solution.py:81
  599.0 7.1 %all-to-all-start.5 = ((f32[128,1,512]{2,1,0:T(1,128)}), f32[128,1,512]{2,1,0:T(1,128)S(1)}, u32[]{:S(2)}, u32[]{:S(2)}) async-start(f32[128,1,512]{2,1,0:T(1,128)} %copy.40), calls=%async_computation.5 | async-start | bytes 524288 | tf_op jit(solution)/shard_map/all_to_all | solution.py:81
  606.3 22.3 %all-to-all-done.5 = f32[128,1,512]{2,1,0:T(1,128)S(1)} async-done(((f32[128,1,512]{2,1,0:T(1,128)}), f32[128,1,512]{2,1,0:T(1,128)S(1)}, u32[]{:S(2)}, u32[]{:S(2)}) %all-to-all-start.5) | async-done | bytes 262176 | tf_op jit(solution)/shard_map/all_to_all | solution.py:81
  629.6 4.3 collective-permute-start.1
  633.9 11.6 %all_gather.3 = bf16[128,2048]{1,0:T(8,128)(2,1)S(1)} all-gather(bf16[128,512]{1,0:T(8,128)(2,1)S(1)} %get-tuple-element.19), channel_id=1, replica_groups=mesh['seq'=128,'ch'=4] {'ch'}, dimensions={1}, use_global_device_ids=true | all-gather | bytes 655360 | tf_op jit(solution)/shard_map/all_gather | solution.py:109
  (98 shorter events, 65.1 us)
Async XLA Ops:
  13.1 11.4 %copy-start.15 = (f32[3,3,512]{2,1,0:T(4,128)S(1)}, f32[3,3,512]{2,1,0:T(4,128)}, u32[]{:S(2)}) copy-start(f32[3,3,512]{2,1,0:T(4,128)} %param.9) | copy-start | bytes 55300
  13.1 24.1 %all-to-all-start.7 = ((bf16[4,512,512]{2,1,0:T(8,128)(2,1)}), bf16[4,512,512]{2,1,0:T(8,128)(2,1)S(1)}, u32[]{:S(2)}, u32[]{:S(2)}) async-start(bf16[4,512,512]{2,1,0:T(8,128)(2,1)} %bitcast.206), calls=%async_computation.7 | async-start | bytes 4194304 | tf_op jit(solution)/shard_map/all_to_all | solution.py:116
  17.6 7.7 %collective-permute-start = (bf16[3,2,512]{2,1,0:T(2,128)(2,1)S(1)}, bf16[3,2,512]{2,1,0:T(2,128)(2,1)S(1)}, u32[]{:S(2)}, u32[]{:S(2)}) collective-permute-start(bf16[3,2,512]{2,1,0:T(2,128)(2,1)S(1)} %slice.59), channel_id=1, source_target_pairs={{0,4},{4,8},{8,12},{12,16},{16,20},{20,24},{24,28},{28,32},{32,36}... | collective-permute-start | bytes 18440 | tf_op jit(solution)/shard_map/ppermute | solution.py:14
  38.0 0.7 copy-start.7
  38.7 28.7 %copy-start.14 = (f32[128,512]{1,0:T(8,128)S(1)}, f32[128,512]{1,0:T(8,128)}, u32[]{:S(2)}) copy-start(f32[128,512]{1,0:T(8,128)} %param.7) | copy-start | bytes 786436
  38.8 51.0 %copy-start.5 = (f32[128,512]{1,0:T(8,128)}, f32[128,512]{1,0:T(8,128)S(1)}, u32[]{:S(2)}) copy-start(f32[128,512]{1,0:T(8,128)S(1)} %get-tuple-element.22) | copy-start | bytes 786436
  39.8 50.1 %all-to-all-start.8 = ((f32[1,128,512]{2,0,1:T(1,128)}), f32[1,128,512]{2,0,1:T(1,128)S(1)}, u32[]{:S(2)}, u32[]{:S(2)}) async-start(f32[1,128,512]{2,0,1:T(1,128)} %copy.41), calls=%async_computation.8 | async-start | bytes 524288 | tf_op jit(solution)/shard_map/all_to_all | solution.py:35
  89.9 40.7 %all-to-all-start = ((f32[1,128,1024]{2,0,1:T(1,128)}), f32[1,128,1024]{2,0,1:T(1,128)S(1)}, u32[]{:S(2)}, u32[]{:S(2)}) async-start(f32[1,128,1024]{2,0,1:T(1,128)} %copy.33), calls=%async_computation | async-start | bytes 1048576 | tf_op jit(solution)/shard_map/all_to_all | solution.py:35
  130.6 40.3 %all-to-all-start.9 = ((f32[256,1,512]{2,1,0:T(1,128)}), f32[256,1,512]{2,1,0:T(1,128)S(1)}, u32[]{:S(2)}, u32[]{:S(2)}) async-start(f32[256,1,512]{2,1,0:T(1,128)} %copy.42), calls=%async_computation.9 | async-start | bytes 1048576 | tf_op jit(solution)/shard_map/all_to_all | solution.py:47
  170.9 40.3 %all-to-all-start.10 = ((f32[256,1,512]{2,1,0:T(1,128)}), f32[256,1,512]{2,1,0:T(1,128)S(1)}, u32[]{:S(2)}, u32[]{:S(2)}) async-start(f32[256,1,512]{2,1,0:T(1,128)} %copy.44), calls=%async_computation.10 | async-start | bytes 1048576 | tf_op jit(solution)/shard_map/all_to_all | solution.py:48
  211.3 9.7 %copy-start.9 = (f32[256,1,512]{2,1,0:T(1,128)}, f32[256,1,512]{2,1,0:T(1,128)S(1)}, u32[]{:S(2)}) copy-start(f32[256,1,512]{2,1,0:T(1,128)S(1)} %all-to-all-done.10) | copy-start | bytes 1572868
  211.3 61.7 %all-to-all-start.1 = ((f32[256,1,1024]{2,1,0:T(1,128)}), f32[256,1,1024]{2,1,0:T(1,128)}, u32[]{:S(2)}, u32[]{:S(2)}) async-start(f32[256,1,1024]{2,1,0:T(1,128)} %copy.34), calls=%async_computation.1 | async-start | bytes 2097152 | tf_op jit(solution)/shard_map/all_to_all | solution.py:47
  272.9 9.5 %copy-start.10 = (f32[256,1,512]{2,1,0:T(1,128)S(1)}, f32[256,1,512]{2,1,0:T(1,128)}, u32[]{:S(2)}) copy-start(f32[256,1,512]{2,1,0:T(1,128)} %copy-done.9) | copy-start | bytes 1572868
  272.9 63.1 %all-to-all-start.2 = ((f32[256,1,1024]{2,1,0:T(1,128)}), f32[256,1,1024]{2,1,0:T(1,128)}, u32[]{:S(2)}, u32[]{:S(2)}) async-start(f32[256,1,1024]{2,1,0:T(1,128)} %copy.36), calls=%async_computation.2 | async-start | bytes 2097152 | tf_op jit(solution)/shard_map/all_to_all | solution.py:48
  338.5 1.2 copy-start.2
  341.0 1.3 copy-start.12
  341.0 1.3 copy-start.13
  346.7 13.2 %copy-start.1 = (f32[2,128,512]{1,2,0:T(8,128)S(1)}, f32[2,128,512]{1,2,0:T(8,128)}, u32[]{:S(2)}) copy-start(f32[2,128,512]{1,2,0:T(8,128)} %get-tuple-element.8) | copy-start | bytes 1572868
  350.6 42.0 %all-to-all-start.3 = ((f32[2,128,512]{2,0,1:T(2,128)}), f32[2,128,512]{2,0,1:T(2,128)}, u32[]{:S(2)}, u32[]{:S(2)}) async-start(f32[2,128,512]{2,0,1:T(2,128)} %copy.38), calls=%async_computation.3 | async-start | bytes 1048576 | tf_op jit(solution)/shard_map/all_to_all | solution.py:75
  392.5 61.5 %all-to-all-start.11 = ((f32[2,128,1024]{2,0,1:T(2,128)}), f32[2,128,1024]{2,0,1:T(2,128)S(1)}, u32[]{:S(2)}, u32[]{:S(2)}) async-start(f32[2,128,1024]{2,0,1:T(2,128)} %copy.46), calls=%async_computation.11 | async-start | bytes 2097152 | tf_op jit(solution)/shard_map/all_to_all | solution.py:75
  399.6 62.8 %copy-start.11 = (f32[2,128,512]{1,2,0:T(8,128)S(1)}, f32[2,128,512]{1,2,0:T(8,128)}, u32[]{:S(2)}) copy-start(f32[2,128,512]{1,2,0:T(8,128)} %get-tuple-element.17) | copy-start | bytes 1572868
  454.0 62.8 %all-to-all-start.12 = ((f32[2,128,1024]{2,0,1:T(2,128)}), f32[2,128,1024]{2,0,1:T(2,128)S(1)}, u32[]{:S(2)}, u32[]{:S(2)}) async-start(f32[2,128,1024]{2,0,1:T(2,128)} %copy.47), calls=%async_computation.12 | async-start | bytes 2097152 | tf_op jit(solution)/shard_map/all_to_all | solution.py:76
  516.8 41.9 %all-to-all-start.4 = ((f32[2,128,512]{2,0,1:T(2,128)}), f32[2,128,512]{2,0,1:T(2,128)S(1)}, u32[]{:S(2)}, u32[]{:S(2)}) async-start(f32[2,128,512]{2,0,1:T(2,128)} %copy.39), calls=%async_computation.4 | async-start | bytes 1048576 | tf_op jit(solution)/shard_map/all_to_all | solution.py:76
  527.3 1.7 copy-start.3
  529.0 1.2 copy-start.4
  558.7 40.3 %all-to-all-start.13 = ((f32[128,1,1024]{2,1,0:T(1,128)}), f32[128,1,1024]{2,1,0:T(1,128)S(1)}, u32[]{:S(2)}, u32[]{:S(2)}) async-start(f32[128,1,1024]{2,1,0:T(1,128)} %copy.48), calls=%async_computation.13 | async-start | bytes 1048576 | tf_op jit(solution)/shard_map/all_to_all | solution.py:81
  567.6 61.0 %copy-start.6 = (f32[128,512]{1,0:T(8,128)S(1)}, f32[128,512]{1,0:T(8,128)}, u32[]{:S(2)}) copy-start(f32[128,512]{1,0:T(8,128)} %copy-done.5) | copy-start | bytes 786436
  567.6 61.0 %copy-start.8 = (f32[128,512]{1,0:T(8,128)S(1)}, f32[128,512]{1,0:T(8,128)}, u32[]{:S(2)}) copy-start(f32[128,512]{1,0:T(8,128)} %copy-done.7) | copy-start | bytes 786436
  567.6 61.0 %copy-start.16 = (f32[512]{0:T(512)S(1)}, f32[512]{0:T(512)}, u32[]{:S(2)}) copy-start(f32[512]{0:T(512)} %param.8) | copy-start | bytes 6148
  599.0 29.5 %all-to-all-start.5 = ((f32[128,1,512]{2,1,0:T(1,128)}), f32[128,1,512]{2,1,0:T(1,128)S(1)}, u32[]{:S(2)}, u32[]{:S(2)}) async-start(f32[128,1,512]{2,1,0:T(1,128)} %copy.40), calls=%async_computation.5 | async-start | bytes 524288 | tf_op jit(solution)/shard_map/all_to_all | solution.py:81
  629.5 16.0 %copy-start = (bf16[2048,512]{1,0:T(8,128)(2,1)S(1)}, bf16[2048,512]{1,0:T(8,128)(2,1)}, u32[]{:S(2)}) copy-start(bf16[2048,512]{1,0:T(8,128)(2,1)} %param.10) | copy-start | bytes 6291460
  629.6 17.0 %collective-permute-start.1 = (f32[3,2,512]{2,1,0:T(2,128)S(1)}, f32[3,2,512]{2,1,0:T(2,128)S(1)}, u32[]{:S(2)}, u32[]{:S(2)}) collective-permute-start(f32[3,2,512]{2,1,0:T(2,128)S(1)} %slice.85), channel_id=1, source_target_pairs={{4,0},{8,4},{12,8},{16,12},{20,16},{24,20},{28,24},{32,28},{36,32}... | collective-permute-start | bytes 36872 | tf_op jit(solution)/shard_map/ppermute | solution.py:14
